TPU v7x, 128 devices: a whole 4x4x4 slice. The times are simulated.
128 devices in a mesh: row: 8 (over z, core), col: 16 (over y, x).
Axes of the slice: x: 4, y: 4, z: 4, core: 2. Of those that a mesh axis runs over, the one named last changes fastest.
Arguments:
- snapshots: bfloat16 [4096, 32768], P('row', 'col'), may hold values from -14 to 14
- neighbours: int32 [4096, 128], P('row'), may hold values from 0 to 4095, all different within a row
- start_basis: float32 [32, 4096], replicated, may hold values from -6 to 6
Outputs:
- basis: float32 [32, 4096], P(None, 'row')
- rayleigh: float32 [32, 32], replicated
Inputs may be any that keep to these rules, and one draw needn't show every extreme that they name: `neighbours`: each row names 128 different snapshots.
All inputs are finite; a program needn't handle non-finite values.
Results may differ from a plain program's by a relative error of at most 0.00145.
Values may be sent and summed in bfloat16 or wider, within the bound.
No kernel may reach another device: no remote copies, remote signals or barrier semaphores. Data moves between devices by JAX's collectives and lax.ppermute only.
A program may use at most 128 MiB of HBM per device.

v0:
```python
import math
import jax
import jax.numpy as jnp
from jax import lax
from jax.sharding import PartitionSpec as P

FEATURES = 32768
LAGS = 64
ITERS = 2


def global_sum(value):
    return lax.psum(value, ("row", "col"))


def collect(columns):
    return lax.all_gather(columns, ("row", "col"), axis=1, tiled=True)


def shards(snapshots, neighbours, start_basis):
    row_count = lax.axis_size("row")
    col_count = lax.axis_size("col")
    row_at = lax.axis_index("row")
    col_at = lax.axis_index("col")
    lag_count = LAGS
    whole = lax.all_gather(snapshots, "row", axis=0, tiled=True)
    snap_count = whole.shape[0]
    feat_width = whole.shape[1]
    col_block = snap_count // col_count
    row_block = snapshots.shape[0]
    squares = jnp.sum(jnp.square(whole.astype(jnp.float32)), axis=1)
    padded_rows = jnp.concatenate([jnp.zeros((lag_count, feat_width), whole.dtype), whole], 0)
    padded_norms = jnp.concatenate([jnp.zeros((lag_count,), jnp.float32), squares], 0)
    row_start = row_at * row_block
    ext_rows = lax.dynamic_slice_in_dim(padded_rows, row_start, row_block + lag_count, 0)
    ext_norms = lax.dynamic_slice_in_dim(padded_norms, row_start, row_block + lag_count, 0)
    row_times = row_start - lag_count + jnp.arange(row_block + lag_count, dtype=jnp.int32)
    span = col_block + lag_count
    blocks = whole.reshape(col_count, col_block, feat_width)
    earlier = jnp.concatenate(
        [jnp.zeros((1, lag_count, feat_width), whole.dtype), blocks[:-1, col_block - lag_count :]],
        0,
    )
    source_rows = jnp.concatenate([earlier, blocks], 1).reshape(col_count * span, feat_width)
    norm_blocks = squares.reshape(col_count, col_block)
    norm_earlier = jnp.concatenate(
        [jnp.zeros((1, lag_count), jnp.float32), norm_blocks[:-1, col_block - lag_count :]], 0
    )
    source_norms = jnp.concatenate([norm_earlier, norm_blocks], 1).reshape(col_count * span)
    virtual = jnp.arange(span * lax.axis_size("col"), dtype=jnp.int32)
    times = virtual // span * col_block + virtual % span - lag_count
    inner = lax.dot_general(
        source_rows, ext_rows, (((1,), (1,)), ((), ())), preferred_element_type=jnp.float32
    )
    term = source_norms[:, None] + ext_norms[None, :] - 2.0 * inner
    keep = (times >= 0)[:, None] & (row_times >= 0)[None, :]
    tile = lax.psum_scatter(
        jnp.where(keep, term, 0.0).astype(jnp.bfloat16), "col", scatter_dimension=0, tiled=True
    ).astype(jnp.float32)
    window = 1
    while window < lag_count:
        tile = tile[window:, window:] + tile[:-window, :-window]
        window = window * 2
    lagged = tile[1:, 1:]
    step_rows = math.gcd(row_block, 16)
    block_count = row_block // step_rows
    slot_count = neighbours.shape[1]
    offset = neighbours - col_at * col_block
    inside = (offset >= 0) & (offset < col_block)
    tile_positions = jnp.arange(col_block, dtype=jnp.int32)

    def pick_block(pair):
        offs, lag_rows = pair
        match = offs[:, :, None] == tile_positions[None, None, :]
        return jnp.sum(jnp.where(match, lag_rows[:, None, :], 0.0), axis=2)

    chosen = lax.map(
        pick_block,
        (
            offset.reshape(block_count, step_rows, slot_count),
            lagged.T.reshape(block_count, step_rows, col_block),
        ),
    )
    chosen = chosen.reshape(row_block, slot_count)
    kernel_part = jnp.where(inside, 1.0 / (1.0 + chosen / (LAGS * FEATURES)), 0.0)
    slot_kernel = lax.psum(kernel_part, "col")
    mass = jnp.sum(slot_kernel, axis=1)
    markov = slot_kernel / mass[:, None]
    snap_positions = jnp.arange(snap_count, dtype=jnp.int32)

    def operator_block(pair):
        ids, weights = pair
        match = ids[:, :, None] == snap_positions[None, None, :]
        return jnp.sum(jnp.where(match, weights[:, :, None], 0.0), axis=1)

    transition = lax.map(
        operator_block,
        (
            neighbours.reshape(block_count, step_rows, slot_count),
            markov.reshape(block_count, step_rows, slot_count),
        ),
    )
    transition = transition.reshape(row_block, snap_count)
    piece_width = snap_count // (row_count * col_count)

    def apply_rows(basis_rows):
        return lax.dot_general(
            basis_rows,
            transition,
            (((1,), (1,)), ((), ())),
            precision=lax.Precision.HIGHEST,
            preferred_element_type=jnp.float32,
        )

    def own_piece(image):
        return lax.dynamic_slice_in_dim(image, col_at * piece_width, piece_width, 1)

    basis = start_basis
    for step in range(ITERS):
        piece = own_piece(apply_rows(basis))
        partial_gram = jnp.dot(
            piece, piece.T, precision=lax.Precision.HIGHEST, preferred_element_type=jnp.float32
        )
        gram_small = global_sum(partial_gram) / snap_count
        lower = jnp.linalg.cholesky(gram_small)
        basis = collect(jax.scipy.linalg.solve_triangular(lower, piece, lower=True))
    image_piece = own_piece(apply_rows(basis))
    basis_piece = lax.dynamic_slice_in_dim(
        basis, (row_at * col_count + col_at) * piece_width, piece_width, 1
    )
    partial_ray = jnp.dot(
        basis_piece,
        image_piece.T,
        precision=lax.Precision.HIGHEST,
        preferred_element_type=jnp.float32,
    )
    rayleigh = global_sum(partial_ray) / snap_count
    basis_rows = lax.dynamic_slice_in_dim(basis, row_start, row_block, 1)
    return (basis_rows, rayleigh)


def solution(mesh):
    placed = (P("row", "col"), P("row", None), P())
    return jax.shard_map(
        shards, mesh=mesh, in_specs=placed, out_specs=(P(None, "row"), P()), check_vma=False
    )
```

profile of v0, /device:TPU:1, one launch (start us, length us, event | category | flops | bytes accessed | tf_op | source)
XLA Modules:
  0.0 1007.9 jit_solution(16402256858035387622)
XLA Ops:
  8.0 90.6 %all-gather.2.cloned.1.call-done = bf16[4096,2048]{1,0:T(8,128)(2,1)} async-done(((bf16[512,2048]{1,0:T(8,128)(2,1)}), bf16[4096,2048]{1,0:T(8,128)(2,1)}) %all-gather.2.cloned.1.call-update) | async-done | bytes 16777232 | tf_op jit(solution)/shard_map/all_gather | solution.py:26
  108.7 21.4 %fusion.5 = bf16[16,320,2048]{2,1,0:T(8,128)(2,1)} fusion(bf16[15,64,2048]{2,1,0:T(8,128)(2,1)S(1)} %slice.69, bf16[16,256,2048]{2,1,0:T(8,128)(2,1)} %bitcast.64), kind=kLoop, calls=%fused_computation.15 | loop fusion | flops 62914560 | bytes 41680896 | tf_op jit(solution)/shard_map/concatenate | solution.py:44
  130.2 23.8 %select_convert_fusion = bf16[5120,576]{1,0:T(8,128)(2,1)} fusion(bf16[5120,2048]{1,0:T(8,128)(2,1)} %bitcast.70, f32[576]{0:T(1024)S(1)} %pad_dynamic-slice_fusion.2, f32[5120]{0:T(1024)S(1)} %add.130, pred[576]{0:T(1024)(128)(4,1)S(1)} %add_compare_fusion, pred[5120]{0:T(1024)(128)(4,1)S(1)} %fusion.17, s32[]{:T(128)S(6)} %select_n.56, ...), kind=kOutput, calls=%fused_computation.17 | convolution fusion | flops 12097290240 | bytes 43675460 | tf_op jit(solution)/shard_map/dot_general | solution.py:52
  154.1 80.7 %reduce-scatter.2.cloned.1.call-done = bf16[320,576]{1,0:T(8,128)(2,1)} async-done(((bf16[5120,576]{1,0:T(8,128)(2,1)}), bf16[320,576]{1,0:T(8,128)(2,1)}) %reduce-scatter.2.cloned.1.call-update) | async-done | bytes 368656 | tf_op jit(solution)/shard_map/reduce_scatter | solution.py:57
  238.1 28.1 %while.22 = (s32[]{:T(128)}, f32[32,16,128]{2,1,0:T(8,128)S(1)}, s32[32,16,128]{2,1,0:T(8,128)S(1)}, f32[32,16,256]{2,1,0:T(8,128)S(1)}, s32[]{:T(128)}) while((s32[]{:T(128)}, f32[32,16,128]{2,1,0:T(8,128)S(1)}, s32[32,16,128]{2,1,0:T(8,128)S(1)}, f32[32,16,256]{2,1,0:T(8,128)S(1)}, s32[]{:T(128)}) %tuple.63), condition=%wide.region_4.5_spmd.clone, body=%wide.region_2.4_spmd.clone.sunk | while | flops 1570818 | bytes 98377 | solution.py:77
  267.0 83.3 %all-reduce.6.cloned.1.call-done = f32[512,128]{1,0:T(8,128)} async-done(((f32[512,128]{1,0:T(8,128)}), f32[512,128]{1,0:T(8,128)}) %all-reduce.6.cloned.1.call-update) | async-done | bytes 262160 | tf_op jit(solution)/shard_map/psum | solution.py:86
  352.5 280.2 %while.23 = (s32[]{:T(128)}, f32[32,16,4096]{2,1,0:T(8,128)}, s32[32,16,128]{2,1,0:T(8,128)S(1)}, f32[32,16,128]{2,1,0:T(8,128)S(1)}, s32[]{:T(128)}) while((s32[]{:T(128)}, f32[32,16,4096]{2,1,0:T(8,128)}, s32[32,16,128]{2,1,0:T(8,128)S(1)}, f32[32,16,128]{2,1,0:T(8,128)S(1)}, s32[]{:T(128)}) %tuple.64), condition=%wide.region_9.10_spmd.clone, body=%wide.region_7.9_spmd.clone.sunk | while | flops 25100288 | bytes 836165 | solution.py:96
  361.3 8.0 select_reduce_fusion.6
  370.0 8.0 select_reduce_fusion.6
  378.8 8.0 select_reduce_fusion.6
  387.5 8.0 select_reduce_fusion.6
  396.3 8.0 select_reduce_fusion.6
  405.1 8.0 select_reduce_fusion.6
  413.8 8.0 select_reduce_fusion.6
  422.6 8.0 select_reduce_fusion.6
  431.4 8.0 select_reduce_fusion.6
  632.7 9.2 fusion.46
  642.1 65.8 %psum.29 = f32[32,32]{0,1:T(8,128)S(1)} all-reduce(f32[32,32]{0,1:T(8,128)S(1)} %fusion.36), channel_id=1, replica_groups=mesh['row'=8,'col'=16] {'row','col'}, use_global_device_ids=true, to_apply=%region_10.11 | all-reduce | flops 1024 | bytes 8192 | tf_op jit(solution)/shard_map/psum | solution.py:13
  714.8 63.7 %all_gather.10 = f32[32,4096]{0,1:T(8,128)S(1)} all-gather(f32[32,32]{0,1:T(8,128)S(1)} %fusion.23), channel_id=1, replica_groups=mesh['row'=8,'col'=16] {'row','col'}, dimensions={1}, use_global_device_ids=true | all-gather | bytes 528384 | tf_op jit(solution)/shard_map/all_gather | solution.py:17
  778.6 9.3 fusion.47
  788.1 65.0 %psum.30 = f32[32,32]{0,1:T(8,128)S(1)} all-reduce(f32[32,32]{0,1:T(8,128)S(1)} %fusion.33), channel_id=1, replica_groups=mesh['row'=8,'col'=16] {'row','col'}, use_global_device_ids=true, to_apply=%region_13.16 | all-reduce | flops 1024 | bytes 8192 | tf_op jit(solution)/shard_map/psum | solution.py:13
  860.2 65.1 %all_gather.11 = f32[32,4096]{0,1:T(8,128)S(1)} all-gather(f32[32,32]{0,1:T(8,128)S(1)} %fusion.20), channel_id=1, replica_groups=mesh['row'=8,'col'=16] {'row','col'}, dimensions={1}, use_global_device_ids=true | all-gather | bytes 528384 | tf_op jit(solution)/shard_map/all_gather | solution.py:17
  925.3 9.2 fusion.48
  934.8 65.0 %psum.31 = f32[32,32]{0,1:T(8,128)S(1)} all-reduce(f32[32,32]{0,1:T(8,128)S(1)} %fusion.29), channel_id=1, replica_groups=mesh['row'=8,'col'=16] {'row','col'}, use_global_device_ids=true, to_apply=%region_14.17 | all-reduce | flops 1024 | bytes 8192 | tf_op jit(solution)/shard_map/psum | solution.py:13
  (316 shorter events, 267.2 us)
Async XLA Ops:
  7.2 625.5 %copy-start = (f32[32,4096]{1,0:T(8,128)S(1)}, f32[32,4096]{1,0:T(8,128)}, u32[]{:S(2)}) copy-start(f32[32,4096]{1,0:T(8,128)} %param.12) | copy-start | bytes 1572868
  7.2 91.4 %all-gather.2.cloned.1.call-start = ((), (), s32[]{:S(2)}) async-start(), calls=%async_computation.1 | async-start | bytes 18874368 | tf_op jit(solution)/shard_map/all_gather | solution.py:26
  7.9 226.8 %reduce-scatter.2.cloned.1.call-start = ((), (), s32[]{:S(2)}) async-start(), calls=%async_computation.2 | async-start | bytes 6963200 | tf_op jit(solution)/shard_map/reduce_scatter | solution.py:57
  106.1 24.0 %slice-start = ((s8[16777216]{0:T(1024)(128)(4,1)}), s8[4194304]{0:T(1024)(128)(4,1)S(1)}, s32[]{:S(2)}) async-start(s8[16777216]{0:T(1024)(128)(4,1)} %bitcast.65), calls=%async_computation.4 | async-start | bytes 8388608
  108.7 21.5 %slice-start.1 = ((s8[16777216]{0:T(1024)(128)(4,1)}), s8[4194304]{0:T(1024)(128)(4,1)S(1)}, s32[]{:S(2)}) async-start(s8[16777216]{0:T(1024)(128)(4,1)} %bitcast.65), calls=%async_computation.5 | async-start | bytes 8388608
  108.7 21.4 %slice-start.2 = ((s8[16777216]{0:T(1024)(128)(4,1)}), s8[4194304]{0:T(1024)(128)(4,1)S(1)}, s32[]{:S(2)}) async-start(s8[16777216]{0:T(1024)(128)(4,1)} %bitcast.65), calls=%async_computation.6 | async-start | bytes 8388608
  108.7 21.4 %slice-start.3 = ((s8[16777216]{0:T(1024)(128)(4,1)}), s8[4194304]{0:T(1024)(128)(4,1)S(1)}, s32[]{:S(2)}) async-start(s8[16777216]{0:T(1024)(128)(4,1)} %bitcast.65), calls=%async_computation.7 | async-start | bytes 8388608
  130.1 23.9 %copy-start.1 = (s32[512,128]{1,0:T(8,128)S(1)}, s32[512,128]{1,0:T(8,128)}, u32[]{:S(2)}) copy-start(s32[512,128]{1,0:T(8,128)} %param.11) | copy-start | bytes 786436
  154.0 196.3 %all-reduce.6.cloned.1.call-start = ((), (), s32[]{:S(2)}) async-start(), calls=%async_computation.3 | async-start | bytes 524288 | tf_op jit(solution)/shard_map/psum | solution.py:86
Sparse Core Ops, SparseCore 0:
  9.7 88.8 all-gather.1
  154.1 80.6 reduce-scatter.1
  267.1 83.1 all-reduce.5
where the time goes:
time: 1020 us; the launch traced here: 1010 us
  other arithmetic  330 us (32%)
  blocking collectives  325 us (32%)
  waiting for transfers between devices  255 us (25%)
  matrix products  52.6 us (5%)
  local copies, waits for them, and re-layouts  29.2 us (3%)
  between operations  14.3 us (1%)
    reduce_sum x32, other arithmetic, operator_block(): return jnp.sum(jnp.where(match, weights[:, :, None], 0.0), axis=1)  256 us
    psum x3, blocking collectives, global_sum(): return lax.psum(value, ('row', 'col'))  196 us
    all_gather x2, blocking collectives, collect(): return lax.all_gather(columns, ('row', 'col'), axis=1, tiled=True)  129 us
    all_gather x1, waiting for transfers between devices, shards(): whole = lax.all_gather(snapshots, 'row', axis=0, tiled=True)  90.6 us
    psum x1, waiting for transfers between devices, shards(): slot_kernel = lax.psum(kernel_part, 'col')  83.3 us
    reduce_scatter x1, waiting for transfers between devices, shards(): lax.psum_scatter(jnp.where(keep, term, 0.0).astype(jnp.bfloat16), 'col',...  80.7 us
    dot_general x3, matrix products, apply_rows(): lax.dot_general(basis_rows, transition, (((1,), (1,)), ((), ())), precisi...  27.6 us
    reduce_sum x32, other arithmetic, pick_block(): return jnp.sum(jnp.where(match, lag_rows[:, None, :], 0.0), axis=2)  25.3 us
  transfers between devices with their start and end apart: 3, of which 3 were waited for; matrix products, arithmetic and copies ran while one was open for 0% of the time, Pallas kernels for 0%

commit v1 on v0

--- a/solution.py
+++ b/solution.py
@@ -10,7 +10,7 @@
 
 
 def global_sum(value):
-    return lax.psum(value, ("row", "col"))
+    return lax.psum(lax.psum(value, "row"), "col")
 
 
 def collect(columns):

time: 1020 us -> 1100 us (1.078)
  blocking collectives: 325 us -> 405 us
    psum x3 -> x6, blocking collectives: 196 us -> 245 us  [global_sum(): return lax.psum(lax.psum(value, 'row'), 'col')]
    all_gather x2, blocking collectives: 129 us -> 160 us  [collect(): return lax.all_gather(columns, ('row', 'col'), axis=1, tiled=True)]
where the time goes in v1:
time: 1100 us; the launch traced here: 1090 us
  blocking collectives  405 us (37%)
  other arithmetic  330 us (30%)
  waiting for transfers between devices  255 us (23%)
  matrix products  52.7 us (5%)
  local copies, waits for them, and re-layouts  29.2 us (3%)
  between operations  14.1 us (1%)
    reduce_sum x32, other arithmetic, operator_block(): return jnp.sum(jnp.where(match, weights[:, :, None], 0.0), axis=1)  256 us
    psum x6, blocking collectives, global_sum(): return lax.psum(lax.psum(value, 'row'), 'col')  245 us
    all_gather x2, blocking collectives, collect(): return lax.all_gather(columns, ('row', 'col'), axis=1, tiled=True)  160 us
    all_gather x1, waiting for transfers between devices, shards(): whole = lax.all_gather(snapshots, 'row', axis=0, tiled=True)  90.6 us
    psum x1, waiting for transfers between devices, shards(): slot_kernel = lax.psum(kernel_part, 'col')  83.3 us
    reduce_scatter x1, waiting for transfers between devices, shards(): lax.psum_scatter(jnp.where(keep, term, 0.0).astype(jnp.bfloat16), 'col',...  80.7 us
    dot_general x3, matrix products, apply_rows(): lax.dot_general(basis_rows, transition, (((1,), (1,)), ((), ())), precisi...  27.7 us
    reduce_sum x32, other arithmetic, pick_block(): return jnp.sum(jnp.where(match, lag_rows[:, None, :], 0.0), axis=2)  25.3 us
  transfers between devices with their start and end apart: 3, of which 3 were waited for; matrix products, arithmetic and copies ran while one was open for 0% of the time, Pallas kernels for 0%

profile of v1, /device:TPU:1, one launch (start us, length us, event | category | flops | bytes accessed | tf_op | source)
XLA Modules:
  0.0 1087.8 jit_solution(3759189856232977223)
XLA Ops:
  8.0 90.6 %all-gather.2.cloned.1.call-done = bf16[4096,2048]{1,0:T(8,128)(2,1)} async-done(((bf16[512,2048]{1,0:T(8,128)(2,1)}), bf16[4096,2048]{1,0:T(8,128)(2,1)}) %all-gather.2.cloned.1.call-update) | async-done | bytes 16777232 | tf_op jit(solution)/shard_map/all_gather | solution.py:26
  108.7 21.4 %fusion.5 = bf16[16,320,2048]{2,1,0:T(8,128)(2,1)} fusion(bf16[15,64,2048]{2,1,0:T(8,128)(2,1)S(1)} %slice.69, bf16[16,256,2048]{2,1,0:T(8,128)(2,1)} %bitcast.64), kind=kLoop, calls=%fused_computation.15 | loop fusion | flops 62914560 | bytes 41680896 | tf_op jit(solution)/shard_map/concatenate | solution.py:44
  130.2 23.8 %select_convert_fusion = bf16[5120,576]{1,0:T(8,128)(2,1)} fusion(bf16[5120,2048]{1,0:T(8,128)(2,1)} %bitcast.70, f32[576]{0:T(1024)S(1)} %pad_dynamic-slice_fusion.2, f32[5120]{0:T(1024)S(1)} %add.136, pred[576]{0:T(1024)(128)(4,1)S(1)} %add_compare_fusion, pred[5120]{0:T(1024)(128)(4,1)S(1)} %fusion.17, s32[]{:T(128)S(6)} %select_n.56, ...), kind=kOutput, calls=%fused_computation.17 | convolution fusion | flops 12097290240 | bytes 43675460 | tf_op jit(solution)/shard_map/dot_general | solution.py:52
  154.1 80.7 %reduce-scatter.2.cloned.1.call-done = bf16[320,576]{1,0:T(8,128)(2,1)} async-done(((bf16[5120,576]{1,0:T(8,128)(2,1)}), bf16[320,576]{1,0:T(8,128)(2,1)}) %reduce-scatter.2.cloned.1.call-update) | async-done | bytes 368656 | tf_op jit(solution)/shard_map/reduce_scatter | solution.py:57
  238.2 27.8 %while.22 = (s32[]{:T(128)}, f32[32,16,128]{2,1,0:T(8,128)S(1)}, s32[32,16,128]{2,1,0:T(8,128)S(1)}, f32[32,16,256]{2,1,0:T(8,128)S(1)}, s32[]{:T(128)}) while((s32[]{:T(128)}, f32[32,16,128]{2,1,0:T(8,128)S(1)}, s32[32,16,128]{2,1,0:T(8,128)S(1)}, f32[32,16,256]{2,1,0:T(8,128)S(1)}, s32[]{:T(128)}) %tuple.63), condition=%wide.region_4.5_spmd.clone, body=%wide.region_2.4_spmd.clone.sunk | while | flops 1570818 | bytes 98377 | solution.py:77
  266.8 83.3 %all-reduce.6.cloned.1.call-done = f32[512,128]{1,0:T(8,128)} async-done(((f32[512,128]{1,0:T(8,128)}), f32[512,128]{1,0:T(8,128)}) %all-reduce.6.cloned.1.call-update) | async-done | bytes 262160 | tf_op jit(solution)/shard_map/psum | solution.py:86
  352.3 280.2 %while.23 = (s32[]{:T(128)}, f32[32,16,4096]{2,1,0:T(8,128)}, s32[32,16,128]{2,1,0:T(8,128)S(1)}, f32[32,16,128]{2,1,0:T(8,128)S(1)}, s32[]{:T(128)}) while((s32[]{:T(128)}, f32[32,16,4096]{2,1,0:T(8,128)}, s32[32,16,128]{2,1,0:T(8,128)S(1)}, f32[32,16,128]{2,1,0:T(8,128)S(1)}, s32[]{:T(128)}) %tuple.64), condition=%wide.region_9.10_spmd.clone, body=%wide.region_7.9_spmd.clone.sunk | while | flops 25100288 | bytes 836165 | solution.py:96
  369.9 8.0 select_reduce_fusion.6
  378.6 8.0 select_reduce_fusion.6
  387.4 8.0 select_reduce_fusion.6
  396.1 8.0 select_reduce_fusion.6
  404.9 8.0 select_reduce_fusion.6
  413.6 8.0 select_reduce_fusion.6
  632.5 9.2 fusion.46
  642.0 22.9 %psum.50 = f32[32,32]{0,1:T(8,128)S(1)} all-reduce(f32[32,32]{0,1:T(8,128)S(1)} %fusion.36), channel_id=1, replica_groups=mesh['row'=8,'col'=16] {'row'}, use_global_device_ids=true, to_apply=%region_10.11 | all-reduce | flops 1024 | bytes 8192 | tf_op jit(solution)/shard_map/psum | solution.py:13
  664.9 58.1 %psum.51 = f32[32,32]{0,1:T(8,128)S(1)} all-reduce(f32[32,32]{0,1:T(8,128)S(1)} %psum.50), channel_id=1, replica_groups=mesh['row'=8,'col'=16] {'col'}, use_global_device_ids=true, to_apply=%region_11.12 | all-reduce | flops 1024 | bytes 8192 | tf_op jit(solution)/shard_map/psum | solution.py:13
  730.0 80.1 %all_gather.10 = f32[32,4096]{0,1:T(8,128)S(1)} all-gather(f32[32,32]{0,1:T(8,128)S(1)} %fusion.23), channel_id=1, replica_groups=mesh['row'=8,'col'=16] {'row','col'}, dimensions={1}, use_global_device_ids=true | all-gather | bytes 528384 | tf_op jit(solution)/shard_map/all_gather | solution.py:17
  810.1 9.3 fusion.47
  819.6 23.6 %psum.52 = f32[32,32]{0,1:T(8,128)S(1)} all-reduce(f32[32,32]{0,1:T(8,128)S(1)} %fusion.33), channel_id=1, replica_groups=mesh['row'=8,'col'=16] {'row'}, use_global_device_ids=true, to_apply=%region_14.17 | all-reduce | flops 1024 | bytes 8192 | tf_op jit(solution)/shard_map/psum | solution.py:13
  843.2 58.2 %psum.53 = f32[32,32]{0,1:T(8,128)S(1)} all-reduce(f32[32,32]{0,1:T(8,128)S(1)} %psum.52), channel_id=1, replica_groups=mesh['row'=8,'col'=16] {'col'}, use_global_device_ids=true, to_apply=%region_15.18 | all-reduce | flops 1024 | bytes 8192 | tf_op jit(solution)/shard_map/psum | solution.py:13
  908.5 80.1 %all_gather.11 = f32[32,4096]{0,1:T(8,128)S(1)} all-gather(f32[32,32]{0,1:T(8,128)S(1)} %fusion.20), channel_id=1, replica_groups=mesh['row'=8,'col'=16] {'row','col'}, dimensions={1}, use_global_device_ids=true | all-gather | bytes 528384 | tf_op jit(solution)/shard_map/all_gather | solution.py:17
  988.6 9.3 fusion.48
  998.1 23.6 %psum.54 = f32[32,32]{0,1:T(8,128)S(1)} all-reduce(f32[32,32]{0,1:T(8,128)S(1)} %fusion.29), channel_id=1, replica_groups=mesh['row'=8,'col'=16] {'row'}, use_global_device_ids=true, to_apply=%region_16.19 | all-reduce | flops 1024 | bytes 8192 | tf_op jit(solution)/shard_map/psum | solution.py:13
  1021.6 58.2 %psum.55 = f32[32,32]{0,1:T(8,128)S(1)} all-reduce(f32[32,32]{0,1:T(8,128)S(1)} %psum.54), channel_id=1, replica_groups=mesh['row'=8,'col'=16] {'col'}, use_global_device_ids=true, to_apply=%region_17.20 | all-reduce | flops 1024 | bytes 8192 | tf_op jit(solution)/shard_map/psum | solution.py:13
  (319 shorter events, 291.3 us)
Async XLA Ops:
  7.2 625.4 %copy-start = (f32[32,4096]{1,0:T(8,128)S(1)}, f32[32,4096]{1,0:T(8,128)}, u32[]{:S(2)}) copy-start(f32[32,4096]{1,0:T(8,128)} %param.12) | copy-start | bytes 1572868
  7.2 91.4 %all-gather.2.cloned.1.call-start = ((), (), s32[]{:S(2)}) async-start(), calls=%async_computation.1 | async-start | bytes 18874368 | tf_op jit(solution)/shard_map/all_gather | solution.py:26
  7.9 226.9 %reduce-scatter.2.cloned.1.call-start = ((), (), s32[]{:S(2)}) async-start(), calls=%async_computation.2 | async-start | bytes 6963200 | tf_op jit(solution)/shard_map/reduce_scatter | solution.py:57
  106.1 24.0 %slice-start = ((s8[16777216]{0:T(1024)(128)(4,1)}), s8[4194304]{0:T(1024)(128)(4,1)S(1)}, s32[]{:S(2)}) async-start(s8[16777216]{0:T(1024)(128)(4,1)} %bitcast.65), calls=%async_computation.4 | async-start | bytes 8388608
  108.7 21.5 %slice-start.1 = ((s8[16777216]{0:T(1024)(128)(4,1)}), s8[4194304]{0:T(1024)(128)(4,1)S(1)}, s32[]{:S(2)}) async-start(s8[16777216]{0:T(1024)(128)(4,1)} %bitcast.65), calls=%async_computation.5 | async-start | bytes 8388608
  108.7 21.4 %slice-start.2 = ((s8[16777216]{0:T(1024)(128)(4,1)}), s8[4194304]{0:T(1024)(128)(4,1)S(1)}, s32[]{:S(2)}) async-start(s8[16777216]{0:T(1024)(128)(4,1)} %bitcast.65), calls=%async_computation.6 | async-start | bytes 8388608
  108.7 21.4 %slice-start.3 = ((s8[16777216]{0:T(1024)(128)(4,1)}), s8[4194304]{0:T(1024)(128)(4,1)S(1)}, s32[]{:S(2)}) async-start(s8[16777216]{0:T(1024)(128)(4,1)} %bitcast.65), calls=%async_computation.7 | async-start | bytes 8388608
  130.1 23.9 %copy-start.1 = (s32[512,128]{1,0:T(8,128)S(1)}, s32[512,128]{1,0:T(8,128)}, u32[]{:S(2)}) copy-start(s32[512,128]{1,0:T(8,128)} %param.11) | copy-start | bytes 786436
  154.0 196.2 %all-reduce.6.cloned.1.call-start = ((), (), s32[]{:S(2)}) async-start(), calls=%async_computation.3 | async-start | bytes 524288 | tf_op jit(solution)/shard_map/psum | solution.py:86
Sparse Core Ops, SparseCore 0:
  9.7 88.8 all-gather.1
  154.1 80.6 reduce-scatter.1
  266.9 83.1 all-reduce.5
